TPU v7x, 32 devices: a whole 2x2x4 slice. The times are simulated.
32 devices in a mesh: section: 8 (over z, x), dp: 4 (over y, core).
Axes of the slice: x: 2, y: 2, z: 4, core: 2. Of those that a mesh axis runs over, the one named last changes fastest.
Arguments:
- block_arguments: bfloat16 [2, 4, 1024, 2048], P(None, 'dp', 'section'), may hold values from -6 to 6
- incoming_batches: bfloat16 [2, 4, 128, 2048], P(None, 'dp'), may hold values from -6 to 6
- output_adjoints: bfloat16 [2, 4, 1024, 2048], P(None, 'dp', 'section'), may hold values from -0.125 to 0.125
- objective_adjoints: bfloat16 [2, 4, 128, 2048], P(None, 'dp'), may hold values from -0.125 to 0.125
- kept_block_arguments: bfloat16 [2, 2, 4, 1024, 2048], P(None, None, 'dp', 'section'), may hold values from -6 to 6
- parameter_arrays: bfloat16 [8, 2048, 1536], P('section', 'dp'), may hold values from -0.125 to 0.125
Outputs:
- ahead_out: bfloat16 [2, 4, 1024, 2048], P(None, 'dp', 'section')
- section_grads: float32 [8, 2048, 1536], P('section', 'dp')
All inputs are finite; a program needn't handle non-finite values.
Results may differ from a plain program's by a relative error of at most 0.013.
Values may be sent and summed in bfloat16 or wider, within the bound.
A program may use at most 128 MiB of HBM per device.

v0:
```python
import jax
import jax.numpy as jnp
from jax import lax
from jax.sharding import PartitionSpec as P


def swapped(block, axis, bit):
    count = lax.axis_size(axis)
    route = []
    for low in range(count):
        high = low | 1 << bit
        if high != low and high < count:
            route += [(low, high), (high, low)]
    return lax.ppermute(block, axis, route)


def passed_along(block, axis, distance):
    devices = range(lax.axis_size(axis))
    route = [(i - distance, i) for i in devices if i - distance in devices]
    return lax.ppermute(block, axis, route)


def normalize(row_block):
    values = row_block.astype(jnp.float32)
    inverse = lax.rsqrt(jnp.mean(values * values, axis=-1, keepdims=True) + 1e-06)
    return (values, inverse, (values * inverse).astype(jnp.bfloat16))


def section_forward(row_block, matrix):
    hidden_width = matrix.shape[1] // 3
    values, inverse, normed = normalize(row_block)
    projected = jnp.dot(normed, matrix[:, : 2 * hidden_width], preferred_element_type=jnp.float32)
    gate_part = projected[:, :hidden_width]
    up_part = projected[:, hidden_width:]
    hidden = (gate_part * jax.nn.sigmoid(gate_part) * up_part).astype(jnp.bfloat16)
    branch = lax.dot_general(
        hidden,
        matrix[:, 2 * hidden_width :],
        (((1,), (1,)), ((), ())),
        preferred_element_type=jnp.float32,
    )
    return (values + branch).astype(jnp.bfloat16)


def reverse_parts(row_block, cotangent, matrix, with_input):
    hidden_width = matrix.shape[1] // 3
    values, inverse, normed = normalize(row_block)
    projected = jnp.dot(normed, matrix[:, : 2 * hidden_width], preferred_element_type=jnp.float32)
    gate_part = projected[:, :hidden_width]
    up_part = projected[:, hidden_width:]
    sigmoid_gate = jax.nn.sigmoid(gate_part)
    silu_gate = gate_part * sigmoid_gate
    hidden = (silu_gate * up_part).astype(jnp.bfloat16)
    hidden_grad = jnp.dot(
        cotangent, matrix[:, 2 * hidden_width :], preferred_element_type=jnp.float32
    )
    projected_grad = jnp.concatenate(
        [
            hidden_grad * up_part * sigmoid_gate * (1.0 + gate_part * (1.0 - sigmoid_gate)),
            hidden_grad * silu_gate,
        ],
        axis=1,
    ).astype(jnp.bfloat16)
    pieces = (normed, projected_grad, cotangent, hidden)
    if not with_input:
        return (pieces, None)
    normed_grad = lax.dot_general(
        projected_grad,
        matrix[:, : 2 * hidden_width],
        (((1,), (1,)), ((), ())),
        preferred_element_type=jnp.float32,
    )
    inner_sum = jnp.mean(normed_grad * values, axis=-1, keepdims=True)
    input_grad = (
        cotangent.astype(jnp.float32)
        + inverse * normed_grad
        - values * inverse * inverse * inverse * inner_sum
    )
    return (pieces, input_grad.astype(jnp.bfloat16))


def weight_pieces(piece_list):
    normed = jnp.concatenate([item[0] for item in piece_list], axis=0)
    projected_grad = jnp.concatenate([item[1] for item in piece_list], axis=0)
    cotangent = jnp.concatenate([item[2] for item in piece_list], axis=0)
    hidden = jnp.concatenate([item[3] for item in piece_list], axis=0)
    inward_grad = lax.dot_general(
        normed, projected_grad, (((0,), (0,)), ((), ())), preferred_element_type=jnp.float32
    )
    outward_grad = lax.dot_general(
        cotangent, hidden, (((0,), (0,)), ((), ())), preferred_element_type=jnp.float32
    )
    return (inward_grad, outward_grad)


def on_device(
    block_arguments,
    incoming_batches,
    output_adjoints,
    objective_adjoints,
    kept_block_arguments,
    parameter_arrays,
):
    position = lax.axis_index("section")
    segment_sequence_catalog = lax.axis_size("section")
    bit_count = segment_sequence_catalog.bit_length() - 1
    bit_order = list(range(bit_count))
    own_slice = parameter_arrays[0]
    resident_parameter_array = lax.all_gather(own_slice, "dp", axis=0, tiled=True)
    first_section = position == 0
    last_section = position == segment_sequence_catalog - 1
    mirror_pack = (
        block_arguments[1, 0],
        output_adjoints[1, 0],
        kept_block_arguments[1, 0, 0],
        kept_block_arguments[1, 1, 0],
    )
    for which_bit in bit_order:
        mirror_pack = swapped(
            (mirror_pack[0], mirror_pack[1], mirror_pack[2], mirror_pack[3]), "section", which_bit
        )
    up_input, up_first_cot, up_first_rows, up_second_rows = mirror_pack
    down_ahead = section_forward(block_arguments[0, 0], resident_parameter_array)
    up_ahead = section_forward(up_input, resident_parameter_array)
    down_first_parts, down_backward_flow = reverse_parts(
        kept_block_arguments[0, 0, 0], output_adjoints[0, 0], resident_parameter_array, True
    )
    upward_first_parts, upward_backward_flow = reverse_parts(
        up_first_rows, up_first_cot, resident_parameter_array, True
    )
    arrivals = passed_along(jnp.stack([down_ahead, up_ahead]), "section", 1)
    returns = passed_along(jnp.stack([down_backward_flow, upward_backward_flow]), "section", -1)
    down_next = jnp.where(first_section, incoming_batches[0, 0], arrivals[0])
    up_next = jnp.where(first_section, incoming_batches[1, 0], arrivals[1])
    descending_adjoint = jnp.where(last_section, objective_adjoints[0, 0], returns[0])
    ascending_adjoint = jnp.where(last_section, objective_adjoints[1, 0], returns[1])
    down_out = section_forward(down_next, resident_parameter_array)
    up_out = section_forward(up_next, resident_parameter_array)
    down_second_parts, discarded_value = reverse_parts(
        kept_block_arguments[0, 1, 0], descending_adjoint, resident_parameter_array, False
    )
    upward_second_parts, discarded_second = reverse_parts(
        up_second_rows, ascending_adjoint, resident_parameter_array, False
    )
    inward_grad, outward_grad = weight_pieces(
        [down_first_parts, down_second_parts, upward_first_parts, upward_second_parts]
    )
    inward_sum, outward_sum = (
        lax.psum_scatter(
            inward_grad.astype(jnp.bfloat16), "dp", scatter_dimension=0, tiled=True
        ).astype(jnp.float32),
        lax.psum_scatter(
            outward_grad.astype(jnp.bfloat16), "dp", scatter_dimension=0, tiled=True
        ).astype(jnp.float32),
    )
    for which_bit in bit_order:
        up_out = swapped(up_out, "section", which_bit)
    ahead_out = jnp.stack([down_out, up_out])[:, None]
    return (ahead_out, jnp.concatenate([inward_sum, outward_sum], axis=1)[None])


def solution(mesh):
    in_specs = (
        P(None, "dp", "section", None),
        P(None, "dp", None, None),
        P(None, "dp", "section", None),
        P(None, "dp", None, None),
        P(None, None, "dp", "section", None),
        P("section", "dp", None),
    )
    out_specs = (P(None, "dp", "section", None), P("section", "dp", None))
    return jax.shard_map(
        on_device, mesh=mesh, in_specs=in_specs, out_specs=out_specs, check_vma=False
    )
```

profile of v0, /device:TPU:21, one launch (start us, length us, event | category | flops | bytes accessed | tf_op | source)
XLA Modules:
  0.0 296.2 jit_solution(9755360608661196092)
XLA Ops:
  12.9 9.3 %collective-permute-done.7 = bf16[128,2048]{1,0:T(8,128)(2,1)S(1)} collective-permute-done((bf16[128,2048]{1,0:T(8,128)(2,1)S(1)}, bf16[128,2048]{1,0:T(8,128)(2,1)S(1)}, u32[]{:S(2)}, u32[]{:S(2)}) %collective-permute-start.7) | collective-permute-done | bytes 524320 | tf_op jit(solution)/shard_map/ppermute | solution.py:14
  22.2 1.3 collective-permute-start.8
  23.5 9.9 %collective-permute-done.10 = bf16[128,2048]{1,0:T(8,128)(2,1)} collective-permute-done((bf16[128,2048]{1,0:T(8,128)(2,1)S(1)}, bf16[128,2048]{1,0:T(8,128)(2,1)}, u32[]{:S(2)}, u32[]{:S(2)}) %collective-permute-start.10) | collective-permute-done | bytes 524320 | tf_op jit(solution)/shard_map/ppermute | solution.py:14
  35.0 9.7 %collective-permute-done.13 = bf16[128,2048]{1,0:T(8,128)(2,1)} collective-permute-done((bf16[128,2048]{1,0:T(8,128)(2,1)S(1)}, bf16[128,2048]{1,0:T(8,128)(2,1)}, u32[]{:S(2)}, u32[]{:S(2)}) %collective-permute-start.13) | collective-permute-done | bytes 524320 | tf_op jit(solution)/shard_map/ppermute | solution.py:14
  46.1 2.3 collective-permute-start.12
  49.4 17.5 %collective-permute-done.14 = bf16[128,2048]{1,0:T(8,128)(2,1)} collective-permute-done((bf16[128,2048]{1,0:T(8,128)(2,1)}, bf16[128,2048]{1,0:T(8,128)(2,1)}, u32[]{:S(2)}, u32[]{:S(2)}) %collective-permute-start.14) | collective-permute-done | bytes 524320 | tf_op jit(solution)/shard_map/ppermute | solution.py:14
  68.3 32.5 %collective-permute-done.12 = bf16[128,2048]{1,0:T(8,128)(2,1)S(1)} collective-permute-done((bf16[128,2048]{1,0:T(8,128)(2,1)}, bf16[128,2048]{1,0:T(8,128)(2,1)S(1)}, u32[]{:S(2)}, u32[]{:S(2)}) %collective-permute-start.12) | collective-permute-done | bytes 524320 | tf_op jit(solution)/shard_map/ppermute | solution.py:14
  102.1 3.2 %fusion.141 = f32[128,1024]{1,0:T(8,128)S(1)} fusion(bf16[128,2048]{1,0:T(8,128)(2,1)} %fusion.23, bf16[2048,1536]{1,0:T(8,128)(2,1)} %bitcast.90), kind=kOutput, calls=%fused_computation.200 | convolution fusion | flops 536870912 | bytes 5242880 | tf_op jit(solution)/shard_map/dot_general | solution.py:48
  105.3 6.8 %collective-permute-done.15 = bf16[128,2048]{1,0:T(8,128)(2,1)} collective-permute-done((bf16[128,2048]{1,0:T(8,128)(2,1)}, bf16[128,2048]{1,0:T(8,128)(2,1)}, u32[]{:S(2)}, u32[]{:S(2)}) %collective-permute-start.15) | collective-permute-done | bytes 524320 | tf_op jit(solution)/shard_map/ppermute | solution.py:14
  112.1 2.3 multiply_convert_fusion.9
  114.4 1.6 fusion.45
  117.8 1.6 fusion.36
  119.9 1.6 fusion.73
  121.6 4.1 %collective-permute-start.16 = (bf16[2,128,2048]{2,1,0:T(8,128)(2,1)S(1)}, bf16[2,128,2048]{2,1,0:T(8,128)(2,1)S(1)}, u32[]{:S(2)}, u32[]{:S(2)}) collective-permute-start(bf16[2,128,2048]{2,1,0:T(8,128)(2,1)S(1)} %pad_maximum_fusion.1), channel_id=1, source_target_pairs={{4,0},{8,4},{12,8},{16,12},{20,16},{24,20},{28,24},{5,1},{9,5},{13... | collective-permute-start | bytes 3145736 | tf_op jit(solution)/shard_map/ppermute | solution.py:20
  127.4 18.2 %collective-permute-done.16 = bf16[2,128,2048]{2,1,0:T(8,128)(2,1)S(1)} collective-permute-done((bf16[2,128,2048]{2,1,0:T(8,128)(2,1)S(1)}, bf16[2,128,2048]{2,1,0:T(8,128)(2,1)S(1)}, u32[]{:S(2)}, u32[]{:S(2)}) %collective-permute-start.16) | collective-permute-done | bytes 1048608 | tf_op jit(solution)/shard_map/ppermute | solution.py:20
  146.9 3.8 %convolution_convert_fusion.1 = bf16[2048,512]{1,0:T(8,128)(2,1)} fusion(bf16[128,2048]{1,0:T(8,128)(2,1)S(1)} %get-tuple-element.15, bf16[128,2048]{1,0:T(8,128)(2,1)} %collective-permute-done.15, bf16[128,2048]{1,0:T(8,128)(2,1)S(1)} %get-tuple-element.14, bf16[128,2048]{1,0:T(8,128)(2,1)S(1)} %copy-done.9, bf16[128,512]{1,0:T(8,128)(2,1)S(1)} %get-tuple-element.29, ...), kind=kOutput, calls=%fused_computation.1 | convolution fusion | flops 1085276160 | bytes 4718592 | tf_op jit(solution)/shard_map/dot_general | solution.py:90
  151.0 4.4 %convolution_convert_fusion = bf16[2048,1024]{1,0:T(8,128)(2,1)} fusion(bf16[128,2048]{1,0:T(8,128)(2,1)S(1)} %fusion.35, bf16[128,2048]{1,0:T(8,128)(2,1)S(1)} %copy-done.8, bf16[128,2048]{1,0:T(8,128)(2,1)S(1)} %copy-done.11, bf16[128,2048]{1,0:T(8,128)(2,1)S(1)} %copy-done.7, bf16[128,512]{1,0:T(8,128)(2,1)S(1)} %get-tuple-element.23, ...), kind=kOutput, calls=%fused_computation | convolution fusion | flops 2166358016 | bytes 7340032 | tf_op jit(solution)/shard_map/dot_general | solution.py:87
  156.7 3.2 %collective-permute-start = (bf16[128,2048]{1,0:T(8,128)(2,1)S(1)}, bf16[128,2048]{1,0:T(8,128)(2,1)S(1)}, u32[]{:S(2)}, u32[]{:S(2)}) collective-permute-start(bf16[128,2048]{1,0:T(8,128)(2,1)S(1)} %slice_bitcast_fusion.8), channel_id=1, source_target_pairs={{0,4},{4,0},{8,12},{12,8},{16,20},{20,16},{24,28},{28,24},{1,5},{5... | collective-permute-start | bytes 1572872 | tf_op jit(solution)/shard_map/ppermute | solution.py:14
  160.0 9.1 %collective-permute-done = bf16[128,2048]{1,0:T(8,128)(2,1)S(1)} collective-permute-done((bf16[128,2048]{1,0:T(8,128)(2,1)S(1)}, bf16[128,2048]{1,0:T(8,128)(2,1)S(1)}, u32[]{:S(2)}, u32[]{:S(2)}) %collective-permute-start) | collective-permute-done | bytes 524320 | tf_op jit(solution)/shard_map/ppermute | solution.py:14
  169.9 9.0 %collective-permute-done.1 = bf16[128,2048]{1,0:T(8,128)(2,1)S(1)} collective-permute-done((bf16[128,2048]{1,0:T(8,128)(2,1)S(1)}, bf16[128,2048]{1,0:T(8,128)(2,1)S(1)}, u32[]{:S(2)}, u32[]{:S(2)}) %collective-permute-start.1) | collective-permute-done | bytes 524320 | tf_op jit(solution)/shard_map/ppermute | solution.py:14
  180.3 21.3 %collective-permute-done.2 = bf16[128,2048]{1,0:T(8,128)(2,1)S(1)} collective-permute-done((bf16[128,2048]{1,0:T(8,128)(2,1)S(1)}, bf16[128,2048]{1,0:T(8,128)(2,1)S(1)}, u32[]{:S(2)}, u32[]{:S(2)}) %collective-permute-start.2) | collective-permute-done | bytes 524320 | tf_op jit(solution)/shard_map/ppermute | solution.py:14
  201.9 3.1 %fusion.71 = f32[128,1024]{1,0:T(8,128)S(1)} fusion(bf16[128,2048]{1,0:T(8,128)(2,1)S(1)} %collective-permute-done.2, f32[128]{0:T(128)S(1)} %add_rsqrt_fusion.6, bf16[2048,1536]{1,0:T(8,128)(2,1)} %bitcast.92), kind=kOutput, calls=%fused_computation.96 | convolution fusion | flops 537657344 | bytes 5243392 | tf_op jit(solution)/shard_map/dot_general | solution.py:32
  205.0 2.4 fusion.5
  209.1 2.5 collective-permute-start.3
  211.7 23.1 %collective-permute-done.3 = bf16[2,128,2048]{2,1,0:T(8,128)(2,1)S(1)} collective-permute-done((bf16[2,128,2048]{2,1,0:T(8,128)(2,1)S(1)}, bf16[2,128,2048]{2,1,0:T(8,128)(2,1)S(1)}, u32[]{:S(2)}, u32[]{:S(2)}) %collective-permute-start.3) | collective-permute-done | bytes 1048608 | tf_op jit(solution)/shard_map/ppermute | solution.py:20
  235.3 3.2 %fusion.67 = f32[128,1024]{1,0:T(8,128)S(1)} fusion(bf16[128,2048]{1,0:T(8,128)(2,1)S(1)} %get-tuple-element.17, f32[128]{0:T(128)S(1)} %add_rsqrt_fusion.4, bf16[2048,1536]{1,0:T(8,128)(2,1)} %bitcast.94), kind=kOutput, calls=%fused_computation.94 | convolution fusion | flops 537657344 | bytes 5243392 | tf_op jit(solution)/shard_map/dot_general | solution.py:32
  238.5 2.4 fusion.3
  241.0 10.8 %collective-permute-done.4 = bf16[128,2048]{1,0:T(8,128)(2,1)S(1)} collective-permute-done((bf16[128,2048]{1,0:T(8,128)(2,1)S(1)}, bf16[128,2048]{1,0:T(8,128)(2,1)S(1)}, u32[]{:S(2)}, u32[]{:S(2)}) %collective-permute-start.4) | collective-permute-done | bytes 524320 | tf_op jit(solution)/shard_map/ppermute | solution.py:14
  252.7 9.0 %collective-permute-done.5 = bf16[128,2048]{1,0:T(8,128)(2,1)S(1)} collective-permute-done((bf16[128,2048]{1,0:T(8,128)(2,1)S(1)}, bf16[128,2048]{1,0:T(8,128)(2,1)S(1)}, u32[]{:S(2)}, u32[]{:S(2)}) %collective-permute-start.5) | collective-permute-done | bytes 524320 | tf_op jit(solution)/shard_map/ppermute | solution.py:14
  261.7 1.7 collective-permute-start.6
  265.0 20.2 %collective-permute-done.6 = bf16[128,2048]{1,0:T(8,128)(2,1)S(1)} collective-permute-done((bf16[128,2048]{1,0:T(8,128)(2,1)S(1)}, bf16[128,2048]{1,0:T(8,128)(2,1)S(1)}, u32[]{:S(2)}, u32[]{:S(2)}) %collective-permute-start.6) | collective-permute-done | bytes 524320 | tf_op jit(solution)/shard_map/ppermute | solution.py:14
  286.3 3.4 %fusion.21 = f32[1,512,1536]{2,1,0:T(8,128)} fusion(bf16[512,512]{1,0:T(8,128)(2,1)} %reduce-scatter.5.cloned.1.call-done, bf16[512,1024]{1,0:T(8,128)(2,1)} %reduce-scatter.3.cloned.1.call-done), kind=kLoop, calls=%fused_computation.28 | loop fusion | flops 3932160 | bytes 4718592 | tf_op jit(solution)/shard_map/broadcast_in_dim | solution.py:159
  (102 shorter events, 27.0 us)
Async XLA Ops:
  7.2 27.6 %copy-start = (bf16[2,2,1,128,2048]{4,3,2,1,0:T(8,128)(2,1)S(1)}, bf16[2,2,1,128,2048]{4,3,2,1,0:T(8,128)(2,1)}, u32[]{:S(2)}) copy-start(bf16[2,2,1,128,2048]{4,3,2,1,0:T(8,128)(2,1)} %param.10) | copy-start | bytes 6291460
  7.2 94.9 %all-gather.3.cloned.1.call-start = ((), (), s32[]{:S(2)}) async-start(), calls=%async_computation.4 | async-start | bytes 7864320 | tf_op jit(solution)/shard_map/all_gather | solution.py:109
  7.9 278.3 %reduce-scatter.5.cloned.1.call-start = ((), (), s32[]{:S(2)}) async-start(), calls=%async_computation.3 | async-start | bytes 2621440 | tf_op jit(solution)/shard_map/reduce_scatter | solution.py:152
  9.3 13.0 %collective-permute-start.7 = (bf16[128,2048]{1,0:T(8,128)(2,1)S(1)}, bf16[128,2048]{1,0:T(8,128)(2,1)S(1)}, u32[]{:S(2)}, u32[]{:S(2)}) collective-permute-start(bf16[128,2048]{1,0:T(8,128)(2,1)S(1)} %get-tuple-element.13), channel_id=1, source_target_pairs={{0,4},{4,0},{8,12},{12,8},{16,20},{20,16},{24,28},{28,24},{1,5},{5... | collective-permute-start | bytes 1572872 | tf_op jit(solution)/shard_map/ppermute | solution.py:14
  10.5 22.9 %collective-permute-start.10 = (bf16[128,2048]{1,0:T(8,128)(2,1)S(1)}, bf16[128,2048]{1,0:T(8,128)(2,1)}, u32[]{:S(2)}, u32[]{:S(2)}) collective-permute-start(bf16[128,2048]{1,0:T(8,128)(2,1)S(1)} %get-tuple-element.12), channel_id=1, source_target_pairs={{0,4},{4,0},{8,12},{12,8},{16,20},{20,16},{24,28},{28,24},{1,5},{5... | collective-permute-start | bytes 1572872 | tf_op jit(solution)/shard_map/ppermute | solution.py:14
  11.7 33.0 %collective-permute-start.13 = (bf16[128,2048]{1,0:T(8,128)(2,1)S(1)}, bf16[128,2048]{1,0:T(8,128)(2,1)}, u32[]{:S(2)}, u32[]{:S(2)}) collective-permute-start(bf16[128,2048]{1,0:T(8,128)(2,1)S(1)} %get-tuple-element.19), channel_id=1, source_target_pairs={{0,4},{4,0},{8,12},{12,8},{16,20},{20,16},{24,28},{28,24},{1,5},{5... | collective-permute-start | bytes 1572872 | tf_op jit(solution)/shard_map/ppermute | solution.py:14
  22.2 23.8 %collective-permute-start.8 = (bf16[128,2048]{1,0:T(8,128)(2,1)S(1)}, bf16[128,2048]{1,0:T(8,128)(2,1)}, u32[]{:S(2)}, u32[]{:S(2)}) collective-permute-start(bf16[128,2048]{1,0:T(8,128)(2,1)S(1)} %collective-permute-done.7), channel_id=1, source_target_pairs={{0,8},{8,0},{4,12},{12,4},{16,24},{24,16},{20,28},{28,20},{1,9},{9... | collective-permute-start | bytes 1572872 | tf_op jit(solution)/shard_map/ppermute | solution.py:14
  33.5 12.6 %collective-permute-start.11 = (bf16[128,2048]{1,0:T(8,128)(2,1)}, bf16[128,2048]{1,0:T(8,128)(2,1)}, u32[]{:S(2)}, u32[]{:S(2)}) collective-permute-start(bf16[128,2048]{1,0:T(8,128)(2,1)} %collective-permute-done.10), channel_id=1, source_target_pairs={{0,8},{8,0},{4,12},{12,4},{16,24},{24,16},{20,28},{28,20},{1,9},{9... | collective-permute-start | bytes 1572872 | tf_op jit(solution)/shard_map/ppermute | solution.py:14
  44.7 22.2 %collective-permute-start.14 = (bf16[128,2048]{1,0:T(8,128)(2,1)}, bf16[128,2048]{1,0:T(8,128)(2,1)}, u32[]{:S(2)}, u32[]{:S(2)}) collective-permute-start(bf16[128,2048]{1,0:T(8,128)(2,1)} %collective-permute-done.13), channel_id=1, source_target_pairs={{0,8},{8,0},{4,12},{12,4},{16,24},{24,16},{20,28},{28,20},{1,9},{9... | collective-permute-start | bytes 1572872 | tf_op jit(solution)/shard_map/ppermute | solution.py:14
  46.0 22.1 %collective-permute-start.9 = (bf16[128,2048]{1,0:T(8,128)(2,1)}, bf16[128,2048]{1,0:T(8,128)(2,1)S(1)}, u32[]{:S(2)}, u32[]{:S(2)}) collective-permute-start(bf16[128,2048]{1,0:T(8,128)(2,1)} %collective-permute-done.8), channel_id=1, source_target_pairs={{0,16},{16,0},{4,20},{20,4},{8,24},{24,8},{12,28},{28,12},{1,17},{... | collective-permute-start | bytes 1572872 | tf_op jit(solution)/shard_map/ppermute | solution.py:14
  46.1 54.8 %collective-permute-start.12 = (bf16[128,2048]{1,0:T(8,128)(2,1)}, bf16[128,2048]{1,0:T(8,128)(2,1)S(1)}, u32[]{:S(2)}, u32[]{:S(2)}) collective-permute-start(bf16[128,2048]{1,0:T(8,128)(2,1)} %collective-permute-done.11), channel_id=1, source_target_pairs={{0,16},{16,0},{4,20},{20,4},{8,24},{24,8},{12,28},{28,12},{1,17},{... | collective-permute-start | bytes 1572872 | tf_op jit(solution)/shard_map/ppermute | solution.py:14
  66.9 45.2 %collective-permute-start.15 = (bf16[128,2048]{1,0:T(8,128)(2,1)}, bf16[128,2048]{1,0:T(8,128)(2,1)}, u32[]{:S(2)}, u32[]{:S(2)}) collective-permute-start(bf16[128,2048]{1,0:T(8,128)(2,1)} %collective-permute-done.14), channel_id=1, source_target_pairs={{0,16},{16,0},{4,20},{20,4},{8,24},{24,8},{12,28},{28,12},{1,17},{... | collective-permute-start | bytes 1572872 | tf_op jit(solution)/shard_map/ppermute | solution.py:14
  102.0 12.4 %slice-start = ((s8[6291456]{0:T(1024)(128)(4,1)}), s8[4194304]{0:T(1024)(128)(4,1)S(1)}, s32[]{:S(2)}) async-start(s8[6291456]{0:T(1024)(128)(4,1)} %bitcast.96), calls=%async_computation.5 | async-start | bytes 8388608
  102.0 12.4 %slice-start.1 = ((s8[6291456]{0:T(1024)(128)(4,1)}), s8[2097152]{0:T(1024)(128)(4,1)S(1)}, s32[]{:S(2)}) async-start(s8[6291456]{0:T(1024)(128)(4,1)} %bitcast.96), calls=%async_computation.6 | async-start | bytes 4194304
  119.9 6.8 %copy-start.10 = (bf16[128,2048]{1,0:T(8,128)(2,1)}, bf16[128,2048]{1,0:T(8,128)(2,1)S(1)}, u32[]{:S(2)}) copy-start(bf16[128,2048]{1,0:T(8,128)(2,1)S(1)} %get-tuple-element.10) | copy-start | bytes 1572868
  121.6 24.0 %collective-permute-start.16 = (bf16[2,128,2048]{2,1,0:T(8,128)(2,1)S(1)}, bf16[2,128,2048]{2,1,0:T(8,128)(2,1)S(1)}, u32[]{:S(2)}, u32[]{:S(2)}) collective-permute-start(bf16[2,128,2048]{2,1,0:T(8,128)(2,1)S(1)} %pad_maximum_fusion.1), channel_id=1, source_target_pairs={{4,0},{8,4},{12,8},{16,12},{20,16},{24,20},{28,24},{5,1},{9,5},{13... | collective-permute-start | bytes 3145736 | tf_op jit(solution)/shard_map/ppermute | solution.py:20
  126.6 19.0 %copy-start.3 = (bf16[2,1,128,2048]{3,2,1,0:T(8,128)(2,1)S(1)}, bf16[2,1,128,2048]{3,2,1,0:T(8,128)(2,1)}, u32[]{:S(2)}) copy-start(bf16[2,1,128,2048]{3,2,1,0:T(8,128)(2,1)} %param.9) | copy-start | bytes 3145732
  146.9 4.1 %copy-start.7 = (bf16[128,2048]{1,0:T(8,128)(2,1)S(1)}, bf16[128,2048]{1,0:T(8,128)(2,1)}, u32[]{:S(2)}) copy-start(bf16[128,2048]{1,0:T(8,128)(2,1)} %fusion.25) | copy-start | bytes 1572868
  146.9 4.1 %copy-start.8 = (bf16[128,2048]{1,0:T(8,128)(2,1)S(1)}, bf16[128,2048]{1,0:T(8,128)(2,1)}, u32[]{:S(2)}) copy-start(bf16[128,2048]{1,0:T(8,128)(2,1)} %fusion.23) | copy-start | bytes 1572868
  150.7 135.5 %reduce-scatter.3.cloned.1.call-start = ((), (), s32[]{:S(2)}) async-start(), calls=%async_computation.2 | async-start | bytes 5242880 | tf_op jit(solution)/shard_map/reduce_scatter | solution.py:149
  156.7 50.7 %slice-start.2 = ((s8[6291456]{0:T(1024)(128)(4,1)}), s8[4194304]{0:T(1024)(128)(4,1)S(1)}, s32[]{:S(2)}) async-start(s8[6291456]{0:T(1024)(128)(4,1)} %bitcast.106), calls=%async_computation.7 | async-start | bytes 8388608
  156.7 12.3 %collective-permute-start = (bf16[128,2048]{1,0:T(8,128)(2,1)S(1)}, bf16[128,2048]{1,0:T(8,128)(2,1)S(1)}, u32[]{:S(2)}, u32[]{:S(2)}) collective-permute-start(bf16[128,2048]{1,0:T(8,128)(2,1)S(1)} %slice_bitcast_fusion.8), channel_id=1, source_target_pairs={{0,4},{4,0},{8,12},{12,8},{16,20},{20,16},{24,28},{28,24},{1,5},{5... | collective-permute-start | bytes 1572872 | tf_op jit(solution)/shard_map/ppermute | solution.py:14
  169.0 9.8 %collective-permute-start.1 = (bf16[128,2048]{1,0:T(8,128)(2,1)S(1)}, bf16[128,2048]{1,0:T(8,128)(2,1)S(1)}, u32[]{:S(2)}, u32[]{:S(2)}) collective-permute-start(bf16[128,2048]{1,0:T(8,128)(2,1)S(1)} %collective-permute-done), channel_id=1, source_target_pairs={{0,8},{8,0},{4,12},{12,4},{16,24},{24,16},{20,28},{28,20},{1,9},{9... | collective-permute-start | bytes 1572872 | tf_op jit(solution)/shard_map/ppermute | solution.py:14
  178.8 22.8 %collective-permute-start.2 = (bf16[128,2048]{1,0:T(8,128)(2,1)S(1)}, bf16[128,2048]{1,0:T(8,128)(2,1)S(1)}, u32[]{:S(2)}, u32[]{:S(2)}) collective-permute-start(bf16[128,2048]{1,0:T(8,128)(2,1)S(1)} %collective-permute-done.1), channel_id=1, source_target_pairs={{0,16},{16,0},{4,20},{20,4},{8,24},{24,8},{12,28},{28,12},{1,17},{... | collective-permute-start | bytes 1572872 | tf_op jit(solution)/shard_map/ppermute | solution.py:14
  201.9 5.6 %slice-start.3 = ((s8[6291456]{0:T(1024)(128)(4,1)}), s8[2097152]{0:T(1024)(128)(4,1)S(1)}, s32[]{:S(2)}) async-start(s8[6291456]{0:T(1024)(128)(4,1)} %bitcast.106), calls=%async_computation.8 | async-start | bytes 4194304
  208.2 26.6 %copy-start.5 = (bf16[2,1,128,2048]{3,2,1,0:T(8,128)(2,1)S(1)}, bf16[2,1,128,2048]{3,2,1,0:T(8,128)(2,1)}, u32[]{:S(2)}) copy-start(bf16[2,1,128,2048]{3,2,1,0:T(8,128)(2,1)} %param.7) | copy-start | bytes 3145732
  209.1 25.7 %collective-permute-start.3 = (bf16[2,128,2048]{2,1,0:T(8,128)(2,1)S(1)}, bf16[2,128,2048]{2,1,0:T(8,128)(2,1)S(1)}, u32[]{:S(2)}, u32[]{:S(2)}) collective-permute-start(bf16[2,128,2048]{2,1,0:T(8,128)(2,1)S(1)} %pad_maximum_fusion), channel_id=1, source_target_pairs={{0,4},{4,8},{8,12},{12,16},{16,20},{20,24},{24,28},{1,5},{5,9},{9,... | collective-permute-start | bytes 3145736 | tf_op jit(solution)/shard_map/ppermute | solution.py:20
  234.8 28.6 %slice-start.4 = ((s8[6291456]{0:T(1024)(128)(4,1)}), s8[4194304]{0:T(1024)(128)(4,1)S(1)}, s32[]{:S(2)}) async-start(s8[6291456]{0:T(1024)(128)(4,1)} %bitcast.110), calls=%async_computation.9 | async-start | bytes 8388608
  235.3 28.1 %slice-start.5 = ((s8[6291456]{0:T(1024)(128)(4,1)}), s8[2097152]{0:T(1024)(128)(4,1)S(1)}, s32[]{:S(2)}) async-start(s8[6291456]{0:T(1024)(128)(4,1)} %bitcast.110), calls=%async_computation.10 | async-start | bytes 4194304
  240.9 10.8 %collective-permute-start.4 = (bf16[128,2048]{1,0:T(8,128)(2,1)S(1)}, bf16[128,2048]{1,0:T(8,128)(2,1)S(1)}, u32[]{:S(2)}, u32[]{:S(2)}) collective-permute-start(bf16[128,2048]{1,0:T(8,128)(2,1)S(1)} %fusion.3), channel_id=1, source_target_pairs={{0,4},{4,0},{8,12},{12,8},{16,20},{20,16},{24,28},{28,24},{1,5},{5... | collective-permute-start | bytes 1572872 | tf_op jit(solution)/shard_map/ppermute | solution.py:14
  251.8 9.9 %collective-permute-start.5 = (bf16[128,2048]{1,0:T(8,128)(2,1)S(1)}, bf16[128,2048]{1,0:T(8,128)(2,1)S(1)}, u32[]{:S(2)}, u32[]{:S(2)}) collective-permute-start(bf16[128,2048]{1,0:T(8,128)(2,1)S(1)} %collective-permute-done.4), channel_id=1, source_target_pairs={{0,8},{8,0},{4,12},{12,4},{16,24},{24,16},{20,28},{28,20},{1,9},{9... | collective-permute-start | bytes 1572872 | tf_op jit(solution)/shard_map/ppermute | solution.py:14
  261.7 23.5 %collective-permute-start.6 = (bf16[128,2048]{1,0:T(8,128)(2,1)S(1)}, bf16[128,2048]{1,0:T(8,128)(2,1)S(1)}, u32[]{:S(2)}, u32[]{:S(2)}) collective-permute-start(bf16[128,2048]{1,0:T(8,128)(2,1)S(1)} %collective-permute-done.5), channel_id=1, source_target_pairs={{0,16},{16,0},{4,20},{20,4},{8,24},{24,8},{12,28},{28,12},{1,17},{... | collective-permute-start | bytes 1572872 | tf_op jit(solution)/shard_map/ppermute | solution.py:14
  (8 other events, 19.1 us)
Sparse Core Ops, SparseCore 0:
  9.6 46.8 all-gather.2
  150.9 34.8 reduce-scatter.4
  188.2 44.5 reduce-scatter.2
where the time goes:
time: 302 us; the launch traced here: 296 us
  waiting for transfers between devices  207 us (69%)
  matrix products  34.9 us (12%)
  starting transfers between devices  25.2 us (8%)
  between operations  14.2 us (5%)
  other arithmetic  10.5 us (3%)
  local copies, waits for them, and re-layouts  3.97 us (1%)
    ppermute x15, waiting for transfers between devices, swapped(): return lax.ppermute(block, axis, route)  165 us
    ppermute x2, waiting for transfers between devices, passed_along(): return lax.ppermute(block, axis, route)  41.4 us
    ppermute x15, starting transfers between devices, swapped(): return lax.ppermute(block, axis, route)  18.3 us
    dot_general x4, matrix products, section_forward(): jnp.dot(normed, matrix[:, :2 * hidden_width], preferred_element_type=jnp....  7.85 us
    ppermute x2, starting transfers between devices, passed_along(): return lax.ppermute(block, axis, route)  6.67 us
    dot_general x4, matrix products, section_forward(): lax.dot_general(hidden, matrix[:, 2 * hidden_width:], (((1,), (1,)), ((),...  6.47 us
  transfers between devices with their start and end apart: 20, of which 14 were waited for; matrix products, arithmetic and copies ran while one was open for 10% of the time, Pallas kernels for 0%

commit v1 on v0

--- a/solution.py
+++ b/solution.py
@@ -4,14 +4,9 @@
 from jax.sharding import PartitionSpec as P
 
 
-def swapped(block, axis, bit):
+def mirrored(block, axis):
     count = lax.axis_size(axis)
-    route = []
-    for low in range(count):
-        high = low | 1 << bit
-        if high != low and high < count:
-            route += [(low, high), (high, low)]
-    return lax.ppermute(block, axis, route)
+    return lax.ppermute(block, axis, [(i, count - 1 - i) for i in range(count)])
 
 
 def passed_along(block, axis, distance):
@@ -103,23 +98,14 @@
 ):
     position = lax.axis_index("section")
     segment_sequence_catalog = lax.axis_size("section")
-    bit_count = segment_sequence_catalog.bit_length() - 1
-    bit_order = list(range(bit_count))
     own_slice = parameter_arrays[0]
     resident_parameter_array = lax.all_gather(own_slice, "dp", axis=0, tiled=True)
     first_section = position == 0
     last_section = position == segment_sequence_catalog - 1
-    mirror_pack = (
-        block_arguments[1, 0],
-        output_adjoints[1, 0],
-        kept_block_arguments[1, 0, 0],
-        kept_block_arguments[1, 1, 0],
-    )
-    for which_bit in bit_order:
-        mirror_pack = swapped(
-            (mirror_pack[0], mirror_pack[1], mirror_pack[2], mirror_pack[3]), "section", which_bit
-        )
-    up_input, up_first_cot, up_first_rows, up_second_rows = mirror_pack
+    up_input = mirrored(block_arguments[1, 0], "section")
+    up_first_rows = mirrored(kept_block_arguments[1, 0, 0], "section")
+    up_first_cot = mirrored(output_adjoints[1, 0], "section")
+    up_second_rows = mirrored(kept_block_arguments[1, 1, 0], "section")
     down_ahead = section_forward(block_arguments[0, 0], resident_parameter_array)
     up_ahead = section_forward(up_input, resident_parameter_array)
     down_first_parts, down_backward_flow = reverse_parts(
@@ -128,8 +114,10 @@
     upward_first_parts, upward_backward_flow = reverse_parts(
         up_first_rows, up_first_cot, resident_parameter_array, True
     )
-    arrivals = passed_along(jnp.stack([down_ahead, up_ahead]), "section", 1)
-    returns = passed_along(jnp.stack([down_backward_flow, upward_backward_flow]), "section", -1)
+    arrivals = [passed_along(item, "section", 1) for item in (down_ahead, up_ahead)]
+    returns = [
+        passed_along(item, "section", -1) for item in (down_backward_flow, upward_backward_flow)
+    ]
     down_next = jnp.where(first_section, incoming_batches[0, 0], arrivals[0])
     up_next = jnp.where(first_section, incoming_batches[1, 0], arrivals[1])
     descending_adjoint = jnp.where(last_section, objective_adjoints[0, 0], returns[0])
@@ -153,8 +141,7 @@
             outward_grad.astype(jnp.bfloat16), "dp", scatter_dimension=0, tiled=True
         ).astype(jnp.float32),
     )
-    for which_bit in bit_order:
-        up_out = swapped(up_out, "section", which_bit)
+    up_out = mirrored(up_out, "section")
     ahead_out = jnp.stack([down_out, up_out])[:, None]
     return (ahead_out, jnp.concatenate([inward_sum, outward_sum], axis=1)[None])
 

time: 302 us -> 227 us (0.75); the launches traced: 296 us -> 226 us
  waiting for transfers between devices: 207 us -> 142 us
  starting transfers between devices: 25.2 us -> 17.4 us
    ppermute x15 -> x5, waiting for transfers between devices: 165 us -> 107 us  [mirrored(): return lax.ppermute(block, axis, [(i, count - 1 - i) for i in range(count)])]
    ppermute x15 -> x5, starting transfers between devices: 18.3 us -> 7.85 us  [mirrored(): return lax.ppermute(block, axis, [(i, count - 1 - i) for i in range(count)])]
    ppermute x2 -> x4, waiting for transfers between devices: 41.4 us -> 34.6 us  [passed_along(): return lax.ppermute(block, axis, route)]
    ppermute x2 -> x4, starting transfers between devices: 6.67 us -> 9.29 us  [passed_along(): return lax.ppermute(block, axis, route)]
  transfers between devices with their start and end apart: 20 -> 12, of which waited for: 14 -> 8; matrix products, arithmetic and copies ran while one was open for 10% -> 19% of each run, Pallas kernels for 0% -> 0%
where the time goes in v1:
time: 227 us; the launch traced here: 226 us
  waiting for transfers between devices  142 us (63%)
  matrix products  36.1 us (16%)
  starting transfers between devices  17.4 us (8%)
  between operations  14.2 us (6%)
  other arithmetic  10.9 us (5%)
  local copies, waits for them, and re-layouts  5.9 us (3%)
    ppermute x5, waiting for transfers between devices, mirrored(): return lax.ppermute(block, axis, [(i, count - 1 - i) for i in range(count)])  107 us
    ppermute x4, waiting for transfers between devices, passed_along(): return lax.ppermute(block, axis, route)  34.6 us
    ppermute x4, starting transfers between devices, passed_along(): return lax.ppermute(block, axis, route)  9.29 us
    dot_general x4, matrix products, section_forward(): jnp.dot(normed, matrix[:, :2 * hidden_width], preferred_element_type=jnp....  7.9 us
    ppermute x5, starting transfers between devices, mirrored(): return lax.ppermute(block, axis, [(i, count - 1 - i) for i in range(count)])  7.85 us
    dot_general x4, matrix products, section_forward(): lax.dot_general(hidden, matrix[:, 2 * hidden_width:], (((1,), (1,)), ((),...  6.5 us
    dot_general x4, matrix products, reverse_parts(): jnp.dot(normed, matrix[:, :2 * hidden_width], preferred_element_type=jnp....  5.4 us
    dot_general x4, matrix products, reverse_parts(): jnp.dot(cotangent, matrix[:, 2 * hidden_width:], preferred_element_type=j...  4.99 us
  transfers between devices with their start and end apart: 12, of which 8 were waited for; matrix products, arithmetic and copies ran while one was open for 19% of the time, Pallas kernels for 0%

profile of v1, /device:TPU:21, one launch (start us, length us, event | category | flops | bytes accessed | tf_op | source)
XLA Modules:
  0.0 226.4 jit_solution(2115386564319349945)
XLA Ops:
  8.0 2.3 %slice_bitcast_fusion.2 = (bf16[128,2048]{1,0:T(8,128)(2,1)}, bf16[128,2048]{1,0:T(8,128)(2,1)}) fusion(bf16[2,2,1,128,2048]{4,3,2,1,0:T(8,128)(2,1)} %param.10), kind=kLoop, calls=%fused_computation.107 | loop fusion | bytes 2097152 | tf_op jit(solution)/shard_map/squeeze | solution.py:108
  10.3 1.1 collective-permute-start.4
  11.4 2.3 %slice_bitcast_fusion.1 = (bf16[128,2048]{1,0:T(8,128)(2,1)}, bf16[128,2048]{1,0:T(8,128)(2,1)}) fusion(bf16[2,1,128,2048]{3,2,1,0:T(8,128)(2,1)} %param.8), kind=kLoop, calls=%fused_computation.106 | loop fusion | bytes 2097152 | tf_op jit(solution)/shard_map/squeeze | solution.py:112
  13.6 1.3 collective-permute-start.7
  17.2 40.7 %collective-permute-done.4 = bf16[128,2048]{1,0:T(8,128)(2,1)S(1)} collective-permute-done((bf16[128,2048]{1,0:T(8,128)(2,1)}, bf16[128,2048]{1,0:T(8,128)(2,1)S(1)}, u32[]{:S(2)}, u32[]{:S(2)}) %collective-permute-start.4) | collective-permute-done | bytes 524320 | tf_op jit(solution)/shard_map/ppermute | solution.py:9
  58.1 22.3 %collective-permute-done.5 = bf16[128,2048]{1,0:T(8,128)(2,1)S(1)} collective-permute-done((bf16[128,2048]{1,0:T(8,128)(2,1)}, bf16[128,2048]{1,0:T(8,128)(2,1)S(1)}, u32[]{:S(2)}, u32[]{:S(2)}) %collective-permute-start.5) | collective-permute-done | bytes 524320 | tf_op jit(solution)/shard_map/ppermute | solution.py:9
  82.5 3.2 %fusion.136 = f32[128,1024]{1,0:T(8,128)S(1)} fusion(bf16[128,2048]{1,0:T(8,128)(2,1)} %fusion.23, bf16[2048,1536]{1,0:T(8,128)(2,1)} %bitcast.64), kind=kOutput, calls=%fused_computation.193 | convolution fusion | flops 536870912 | bytes 5242880 | tf_op jit(solution)/shard_map/dot_general | solution.py:43
  85.7 2.4 %multiply_convert_fusion.11 = (bf16[128,512]{1,0:T(8,128)(2,1)S(1)}, bf16[128,512]{1,0:T(8,128)(2,1)S(1)}, bf16[128,512]{1,0:T(8,128)(2,1)S(1)}) fusion(f32[128,1024]{1,0:T(8,128)S(1)} %fusion.136, bf16[2048,1536]{1,0:T(8,128)(2,1)} %bitcast.65, bf16[2,1,128,2048]{3,2,1,0:T(8,128)(2,1)S(1)} %copy-done.1), kind=kOutput, calls=%fused_computation.160 | convolution fusion | flops 269418496 | bytes 3538944 | tf_op jit(solution)/shard_map/dot_general | solution.py:49
  88.2 1.6 fusion.34
  90.3 3.2 %collective-permute-start.6 = (bf16[128,2048]{1,0:T(8,128)(2,1)S(1)}, bf16[128,2048]{1,0:T(8,128)(2,1)S(1)}, u32[]{:S(2)}, u32[]{:S(2)}) collective-permute-start(bf16[128,2048]{1,0:T(8,128)(2,1)S(1)} %get-tuple-element.11), channel_id=1, source_target_pairs={{4,0},{8,4},{12,8},{16,12},{20,16},{24,20},{28,24},{5,1},{9,5},{13... | collective-permute-start | bytes 1572872 | tf_op jit(solution)/shard_map/ppermute | solution.py:15
  94.3 1.6 multiply_convert_fusion.7
  95.9 1.6 fusion.43
  97.5 1.4 fusion.31
  98.9 2.1 collective-permute-start.8
  102.5 1.6 collective-permute-done.6
  104.1 11.2 %collective-permute-done.8 = bf16[128,2048]{1,0:T(8,128)(2,1)S(1)} collective-permute-done((bf16[128,2048]{1,0:T(8,128)(2,1)S(1)}, bf16[128,2048]{1,0:T(8,128)(2,1)S(1)}, u32[]{:S(2)}, u32[]{:S(2)}) %collective-permute-start.8) | collective-permute-done | bytes 524320 | tf_op jit(solution)/shard_map/ppermute | solution.py:15
  116.5 3.8 %convolution_convert_fusion.1 = bf16[2048,512]{1,0:T(8,128)(2,1)} fusion(bf16[128,2048]{1,0:T(8,128)(2,1)S(1)} %get-tuple-element.17, bf16[128,2048]{1,0:T(8,128)(2,1)} %collective-permute-done.7, bf16[128,2048]{1,0:T(8,128)(2,1)S(1)} %get-tuple-element.16, bf16[128,2048]{1,0:T(8,128)(2,1)S(1)} %copy-done.8, bf16[128,512]{1,0:T(8,128)(2,1)S(1)} %get-tuple-element.29, ...), kind=kOutput, calls=%fused_computation.1 | convolution fusion | flops 1085276160 | bytes 4718592 | tf_op jit(solution)/shard_map/dot_general | solution.py:85
  120.6 4.4 %convolution_convert_fusion = bf16[2048,1024]{1,0:T(8,128)(2,1)} fusion(bf16[128,2048]{1,0:T(8,128)(2,1)S(1)} %copy-done.7, bf16[128,2048]{1,0:T(8,128)(2,1)S(1)} %copy-done.6, bf16[128,2048]{1,0:T(8,128)(2,1)S(1)} %copy-done.10, bf16[128,2048]{1,0:T(8,128)(2,1)S(1)} %copy-done.5, bf16[128,512]{1,0:T(8,128)(2,1)S(1)} %get-tuple-element.23, ...), kind=kOutput, calls=%fused_computation | convolution fusion | flops 2166358016 | bytes 7340032 | tf_op jit(solution)/shard_map/dot_general | solution.py:82
  125.0 1.2 copy-done.3
  126.2 2.6 %collective-permute-start.1 = (bf16[128,2048]{1,0:T(8,128)(2,1)S(1)}, bf16[128,2048]{1,0:T(8,128)(2,1)S(1)}, u32[]{:S(2)}, u32[]{:S(2)}) collective-permute-start(bf16[128,2048]{1,0:T(8,128)(2,1)S(1)} %slice_bitcast_fusion.4), channel_id=1, source_target_pairs={{0,28},{4,24},{8,20},{12,16},{16,12},{20,8},{24,4},{28,0},{1,29},{... | collective-permute-start | bytes 1572872 | tf_op jit(solution)/shard_map/ppermute | solution.py:9
  129.0 22.8 %collective-permute-done.1 = bf16[128,2048]{1,0:T(8,128)(2,1)S(1)} collective-permute-done((bf16[128,2048]{1,0:T(8,128)(2,1)S(1)}, bf16[128,2048]{1,0:T(8,128)(2,1)S(1)}, u32[]{:S(2)}, u32[]{:S(2)}) %collective-permute-start.1) | collective-permute-done | bytes 524320 | tf_op jit(solution)/shard_map/ppermute | solution.py:9
  152.0 3.1 %fusion.63 = f32[128,1024]{1,0:T(8,128)S(1)} fusion(f32[128]{0:T(128)S(1)} %add_rsqrt_fusion.7, bf16[2,1,128,2048]{3,2,1,0:T(8,128)(2,1)S(1)} %copy-done.3, bf16[2048,1536]{1,0:T(8,128)(2,1)} %bitcast.66), kind=kOutput, calls=%fused_computation.89 | convolution fusion | flops 537657344 | bytes 5243392 | tf_op jit(solution)/shard_map/dot_general | solution.py:27
  155.1 2.4 %fusion = bf16[128,2048]{1,0:T(8,128)(2,1)S(1)} fusion(bf16[2,1,128,2048]{3,2,1,0:T(8,128)(2,1)S(1)} %copy-done.3, bf16[2048,1536]{1,0:T(8,128)(2,1)} %bitcast.67, f32[128,1024]{1,0:T(8,128)S(1)} %fusion.63), kind=kOutput, calls=%fused_computation.6 | convolution fusion | flops 269615104 | bytes 3670016 | tf_op jit(solution)/shard_map/dot_general | solution.py:31
  157.6 2.1 collective-permute-start
  161.2 1.9 collective-permute-start.2
  163.2 10.5 %collective-permute-done = bf16[128,2048]{1,0:T(8,128)(2,1)S(1)} collective-permute-done((bf16[128,2048]{1,0:T(8,128)(2,1)S(1)}, bf16[128,2048]{1,0:T(8,128)(2,1)S(1)}, u32[]{:S(2)}, u32[]{:S(2)}) %collective-permute-start) | collective-permute-done | bytes 524320 | tf_op jit(solution)/shard_map/ppermute | solution.py:15
  173.7 11.2 %collective-permute-done.2 = bf16[128,2048]{1,0:T(8,128)(2,1)S(1)} collective-permute-done((bf16[128,2048]{1,0:T(8,128)(2,1)S(1)}, bf16[128,2048]{1,0:T(8,128)(2,1)S(1)}, u32[]{:S(2)}, u32[]{:S(2)}) %collective-permute-start.2) | collective-permute-done | bytes 524320 | tf_op jit(solution)/shard_map/ppermute | solution.py:15
  185.4 3.2 %fusion.65 = f32[128,1024]{1,0:T(8,128)S(1)} fusion(bf16[128,2048]{1,0:T(8,128)(2,1)S(1)} %get-tuple-element.19, f32[128]{0:T(128)S(1)} %add_rsqrt_fusion.4, bf16[2048,1536]{1,0:T(8,128)(2,1)} %bitcast.68), kind=kOutput, calls=%fused_computation.90 | convolution fusion | flops 537657344 | bytes 5243392 | tf_op jit(solution)/shard_map/dot_general | solution.py:27
  188.7 2.4 %fusion.3 = bf16[128,2048]{1,0:T(8,128)(2,1)S(1)} fusion(bf16[128,2048]{1,0:T(8,128)(2,1)S(1)} %get-tuple-element.19, bf16[2048,1536]{1,0:T(8,128)(2,1)} %bitcast.69, f32[128,1024]{1,0:T(8,128)S(1)} %fusion.65), kind=kOutput, calls=%fused_computation.9 | convolution fusion | flops 269615104 | bytes 3670016 | tf_op jit(solution)/shard_map/dot_general | solution.py:31
  191.1 1.8 collective-permute-start.3
  194.6 20.8 %collective-permute-done.3 = bf16[128,2048]{1,0:T(8,128)(2,1)S(1)} collective-permute-done((bf16[128,2048]{1,0:T(8,128)(2,1)S(1)}, bf16[128,2048]{1,0:T(8,128)(2,1)S(1)}, u32[]{:S(2)}, u32[]{:S(2)}) %collective-permute-start.3) | collective-permute-done | bytes 524320 | tf_op jit(solution)/shard_map/ppermute | solution.py:9
  216.5 3.4 %fusion.19 = f32[1,512,1536]{2,1,0:T(8,128)} fusion(bf16[512,512]{1,0:T(8,128)(2,1)} %reduce-scatter.5.cloned.1.call-done, bf16[512,1024]{1,0:T(8,128)(2,1)} %reduce-scatter.3.cloned.1.call-done), kind=kLoop, calls=%fused_computation.26 | loop fusion | flops 3932160 | bytes 4718592 | tf_op jit(solution)/shard_map/broadcast_in_dim | solution.py:146
  (75 shorter events, 14.6 us)
Async XLA Ops:
  7.2 8.8 %copy-start = (bf16[2,2,1,128,2048]{4,3,2,1,0:T(8,128)(2,1)S(1)}, bf16[2,2,1,128,2048]{4,3,2,1,0:T(8,128)(2,1)}, u32[]{:S(2)}) copy-start(bf16[2,2,1,128,2048]{4,3,2,1,0:T(8,128)(2,1)} %param.10) | copy-start | bytes 6291460
  7.2 75.3 %all-gather.3.cloned.1.call-start = ((), (), s32[]{:S(2)}) async-start(), calls=%async_computation.4 | async-start | bytes 7864320 | tf_op jit(solution)/shard_map/all_gather | solution.py:102
  7.9 208.5 %reduce-scatter.5.cloned.1.call-start = ((), (), s32[]{:S(2)}) async-start(), calls=%async_computation.3 | async-start | bytes 2621440 | tf_op jit(solution)/shard_map/reduce_scatter | solution.py:140
  10.3 47.6 %collective-permute-start.4 = (bf16[128,2048]{1,0:T(8,128)(2,1)}, bf16[128,2048]{1,0:T(8,128)(2,1)S(1)}, u32[]{:S(2)}, u32[]{:S(2)}) collective-permute-start(bf16[128,2048]{1,0:T(8,128)(2,1)} %get-tuple-element.13), channel_id=1, source_target_pairs={{0,28},{4,24},{8,20},{12,16},{16,12},{20,8},{24,4},{28,0},{1,29},{... | collective-permute-start | bytes 1572872 | tf_op jit(solution)/shard_map/ppermute | solution.py:9
  13.6 80.7 %collective-permute-start.7 = (bf16[128,2048]{1,0:T(8,128)(2,1)}, bf16[128,2048]{1,0:T(8,128)(2,1)}, u32[]{:S(2)}, u32[]{:S(2)}) collective-permute-start(bf16[128,2048]{1,0:T(8,128)(2,1)} %get-tuple-element.15), channel_id=1, source_target_pairs={{0,28},{4,24},{8,20},{12,16},{16,12},{20,8},{24,4},{28,0},{1,29},{... | collective-permute-start | bytes 1572872 | tf_op jit(solution)/shard_map/ppermute | solution.py:9
  14.9 65.5 %collective-permute-start.5 = (bf16[128,2048]{1,0:T(8,128)(2,1)}, bf16[128,2048]{1,0:T(8,128)(2,1)S(1)}, u32[]{:S(2)}, u32[]{:S(2)}) collective-permute-start(bf16[128,2048]{1,0:T(8,128)(2,1)} %get-tuple-element.12), channel_id=1, source_target_pairs={{0,28},{4,24},{8,20},{12,16},{16,12},{20,8},{24,4},{28,0},{1,29},{... | collective-permute-start | bytes 1572872 | tf_op jit(solution)/shard_map/ppermute | solution.py:9
  82.5 3.2 %copy-start.1 = (bf16[2,1,128,2048]{3,2,1,0:T(8,128)(2,1)S(1)}, bf16[2,1,128,2048]{3,2,1,0:T(8,128)(2,1)}, u32[]{:S(2)}) copy-start(bf16[2,1,128,2048]{3,2,1,0:T(8,128)(2,1)} %param.8) | copy-start | bytes 3145732
  82.5 5.7 %copy-start.11 = (bf16[1,2048,1536]{2,1,0:T(8,128)(2,1)S(1)}, bf16[1,2048,1536]{2,1,0:T(8,128)(2,1)}, u32[]{:S(2)}) copy-start(bf16[1,2048,1536]{2,1,0:T(8,128)(2,1)} %all-gather.3.cloned.1.call-done) | copy-start | bytes 18874372
  88.2 5.4 %copy-start.6 = (bf16[128,2048]{1,0:T(8,128)(2,1)S(1)}, bf16[128,2048]{1,0:T(8,128)(2,1)}, u32[]{:S(2)}) copy-start(bf16[128,2048]{1,0:T(8,128)(2,1)} %fusion.21) | copy-start | bytes 1572868
  90.3 11.5 %copy-start.9 = (bf16[128,2048]{1,0:T(8,128)(2,1)}, bf16[128,2048]{1,0:T(8,128)(2,1)S(1)}, u32[]{:S(2)}) copy-start(bf16[128,2048]{1,0:T(8,128)(2,1)S(1)} %get-tuple-element.10) | copy-start | bytes 1572868
  90.3 13.8 %collective-permute-start.6 = (bf16[128,2048]{1,0:T(8,128)(2,1)S(1)}, bf16[128,2048]{1,0:T(8,128)(2,1)S(1)}, u32[]{:S(2)}, u32[]{:S(2)}) collective-permute-start(bf16[128,2048]{1,0:T(8,128)(2,1)S(1)} %get-tuple-element.11), channel_id=1, source_target_pairs={{4,0},{8,4},{12,8},{16,12},{20,16},{24,20},{28,24},{5,1},{9,5},{13... | collective-permute-start | bytes 1572872 | tf_op jit(solution)/shard_map/ppermute | solution.py:15
  95.9 5.1 %copy-start.7 = (bf16[128,2048]{1,0:T(8,128)(2,1)S(1)}, bf16[128,2048]{1,0:T(8,128)(2,1)}, u32[]{:S(2)}) copy-start(bf16[128,2048]{1,0:T(8,128)(2,1)} %fusion.33) | copy-start | bytes 1572868
  98.9 16.4 %collective-permute-start.8 = (bf16[128,2048]{1,0:T(8,128)(2,1)S(1)}, bf16[128,2048]{1,0:T(8,128)(2,1)S(1)}, u32[]{:S(2)}, u32[]{:S(2)}) collective-permute-start(bf16[128,2048]{1,0:T(8,128)(2,1)S(1)} %fusion.31), channel_id=1, source_target_pairs={{4,0},{8,4},{12,8},{16,12},{20,16},{24,20},{28,24},{5,1},{9,5},{13... | collective-permute-start | bytes 1572872 | tf_op jit(solution)/shard_map/ppermute | solution.py:15
  101.8 13.6 %copy-start.2 = (bf16[2,1,128,2048]{3,2,1,0:T(8,128)(2,1)S(1)}, bf16[2,1,128,2048]{3,2,1,0:T(8,128)(2,1)}, u32[]{:S(2)}) copy-start(bf16[2,1,128,2048]{3,2,1,0:T(8,128)(2,1)} %param.9) | copy-start | bytes 3145732
  115.5 1.0 copy-start.8
  116.5 4.0 %copy-start.5 = (bf16[128,2048]{1,0:T(8,128)(2,1)S(1)}, bf16[128,2048]{1,0:T(8,128)(2,1)}, u32[]{:S(2)}) copy-start(bf16[128,2048]{1,0:T(8,128)(2,1)} %fusion.23) | copy-start | bytes 1572868
  116.5 4.0 %copy-start.10 = (bf16[128,2048]{1,0:T(8,128)(2,1)S(1)}, bf16[128,2048]{1,0:T(8,128)(2,1)}, u32[]{:S(2)}) copy-start(bf16[128,2048]{1,0:T(8,128)(2,1)} %copy-done.9) | copy-start | bytes 1572868
  120.3 96.1 %reduce-scatter.3.cloned.1.call-start = ((), (), s32[]{:S(2)}) async-start(), calls=%async_computation.2 | async-start | bytes 5242880 | tf_op jit(solution)/shard_map/reduce_scatter | solution.py:137
  125.0 1.2 copy-start.3
  126.2 25.5 %collective-permute-start.1 = (bf16[128,2048]{1,0:T(8,128)(2,1)S(1)}, bf16[128,2048]{1,0:T(8,128)(2,1)S(1)}, u32[]{:S(2)}, u32[]{:S(2)}) collective-permute-start(bf16[128,2048]{1,0:T(8,128)(2,1)S(1)} %slice_bitcast_fusion.4), channel_id=1, source_target_pairs={{0,28},{4,24},{8,20},{12,16},{16,12},{20,8},{24,4},{28,0},{1,29},{... | collective-permute-start | bytes 1572872 | tf_op jit(solution)/shard_map/ppermute | solution.py:9
  152.0 7.7 %slice-start = ((s8[6291456]{0:T(1024)(128)(4,1)}), s8[4194304]{0:T(1024)(128)(4,1)S(1)}, s32[]{:S(2)}) async-start(s8[6291456]{0:T(1024)(128)(4,1)} %bitcast.78), calls=%async_computation.5 | async-start | bytes 8388608
  152.0 7.7 %slice-start.1 = ((s8[6291456]{0:T(1024)(128)(4,1)}), s8[2097152]{0:T(1024)(128)(4,1)S(1)}, s32[]{:S(2)}) async-start(s8[6291456]{0:T(1024)(128)(4,1)} %bitcast.78), calls=%async_computation.6 | async-start | bytes 4194304
  157.5 27.4 %copy-start.4 = (bf16[2,1,128,2048]{3,2,1,0:T(8,128)(2,1)S(1)}, bf16[2,1,128,2048]{3,2,1,0:T(8,128)(2,1)}, u32[]{:S(2)}) copy-start(bf16[2,1,128,2048]{3,2,1,0:T(8,128)(2,1)} %param.7) | copy-start | bytes 3145732
  157.6 16.1 %collective-permute-start = (bf16[128,2048]{1,0:T(8,128)(2,1)S(1)}, bf16[128,2048]{1,0:T(8,128)(2,1)S(1)}, u32[]{:S(2)}, u32[]{:S(2)}) collective-permute-start(bf16[128,2048]{1,0:T(8,128)(2,1)S(1)} %fusion), channel_id=1, source_target_pairs={{0,4},{4,8},{8,12},{12,16},{16,20},{20,24},{24,28},{1,5},{5,9},{9,... | collective-permute-start | bytes 1572872 | tf_op jit(solution)/shard_map/ppermute | solution.py:15
  161.2 23.7 %collective-permute-start.2 = (bf16[128,2048]{1,0:T(8,128)(2,1)S(1)}, bf16[128,2048]{1,0:T(8,128)(2,1)S(1)}, u32[]{:S(2)}, u32[]{:S(2)}) collective-permute-start(bf16[128,2048]{1,0:T(8,128)(2,1)S(1)} %fusion.2), channel_id=1, source_target_pairs={{0,4},{4,8},{8,12},{12,16},{16,20},{20,24},{24,28},{1,5},{5,9},{9,... | collective-permute-start | bytes 1572872 | tf_op jit(solution)/shard_map/ppermute | solution.py:15
  184.9 8.0 %slice-start.2 = ((s8[6291456]{0:T(1024)(128)(4,1)}), s8[4194304]{0:T(1024)(128)(4,1)S(1)}, s32[]{:S(2)}) async-start(s8[6291456]{0:T(1024)(128)(4,1)} %bitcast.82), calls=%async_computation.7 | async-start | bytes 8388608
  185.4 7.5 %slice-start.3 = ((s8[6291456]{0:T(1024)(128)(4,1)}), s8[2097152]{0:T(1024)(128)(4,1)S(1)}, s32[]{:S(2)}) async-start(s8[6291456]{0:T(1024)(128)(4,1)} %bitcast.82), calls=%async_computation.8 | async-start | bytes 4194304
  191.1 24.3 %collective-permute-start.3 = (bf16[128,2048]{1,0:T(8,128)(2,1)S(1)}, bf16[128,2048]{1,0:T(8,128)(2,1)S(1)}, u32[]{:S(2)}, u32[]{:S(2)}) collective-permute-start(bf16[128,2048]{1,0:T(8,128)(2,1)S(1)} %fusion.3), channel_id=1, source_target_pairs={{0,28},{4,24},{8,20},{12,16},{16,12},{20,8},{24,4},{28,0},{1,29},{... | collective-permute-start | bytes 1572872 | tf_op jit(solution)/shard_map/ppermute | solution.py:9
Sparse Core Ops, SparseCore 0:
  9.5 46.9 all-gather.2
  120.4 32.6 reduce-scatter.4
  155.7 44.5 reduce-scatter.2

commit v2 on v1

v2 whole, which is shorter than its diff:
```python
import functools

import jax
import jax.numpy as jnp
from jax import lax
from jax.experimental import pallas as pl
from jax.experimental.pallas import tpu as pltpu
from jax.sharding import PartitionSpec as P

MESH = pl.DeviceIdType.MESH
F32, BF16 = jnp.float32, jnp.bfloat16
HALVES = 2
CHUNKS = 2


def tiles_of(total, most):
    size = min(total, most)
    return size, total // size


def kernel(
    n_sec,
    n_dp,
    x_hbm,
    inc_hbm,
    adj_hbm,
    obj_hbm,
    kept_hbm,
    w_hbm,
    ahead_hbm,
    grads_hbm,
    w,
    x4,
    c4,
    k4,
    n4,
    p4,
    h4,
    o6,
    fn,
    fh,
    inv_ref,
    g_ref,
    part_send,
    part_recv,
    own,
    y_send,
    y_recv,
    grad_out,
    local_sem,
    w_send,
    w_recv,
    mir_send,
    mir_recv,
    pass_send,
    pass_recv,
    red_send,
    red_recv,
    out_sem,
):
    s = lax.axis_index("section")
    r = lax.axis_index("dp")
    groups = n_dp // 2
    h, c = r // 2, r % 2
    partner = 2 * h + (1 - c)
    opposite = n_sec - 1 - s
    first, last = s == 0, s == n_sec - 1
    rows = w_hbm.shape[1]
    width = w_hbm.shape[2]
    ff = width // 3
    tokens, features = x_hbm.shape[2], x_hbm.shape[3]

    def remote(src, dst, send, recv, **where):
        return pltpu.make_async_remote_copy(
            src_ref=src,
            dst_ref=dst,
            send_sem=send,
            recv_sem=recv,
            device_id=where,
            device_id_type=MESH,
        )

    def dp_at(j):
        return 2 * lax.rem(h + j, groups) + c

    def span(block, size=tokens):
        return pl.ds(block * size, size)

    barrier = pltpu.get_barrier_semaphore()

    def greet(**where):
        pl.semaphore_signal(barrier, inc=1, device_id=where, device_id_type=MESH)

    greet(section=opposite)
    greet(dp=partner)
    for j in range(1, groups):
        greet(dp=dp_at(j))

    greet(section=lax.rem(s + 1, n_sec))
    greet(section=lax.rem(s + n_sec - 1, n_sec))

    local = [
        pltpu.make_async_copy(w_hbm.at[0], w.at[pl.ds(pl.multiple_of(r * rows, rows), rows)], local_sem.at[0]),
        pltpu.make_async_copy(kept_hbm.at[0, 0, 0], k4.at[span(0)], local_sem.at[1]),
        pltpu.make_async_copy(adj_hbm.at[0, 0], c4.at[span(0)], local_sem.at[2]),
        pltpu.make_async_copy(x_hbm.at[0, 0], x4.at[span(0)], local_sem.at[3]),
        pltpu.make_async_copy(kept_hbm.at[0, 1, 0], k4.at[span(2)], local_sem.at[4]),
    ]
    for copy in local:
        copy.start()
    edge_in = [
        pltpu.make_async_copy(inc_hbm.at[d, 0], x4.at[span(2 + d)], local_sem.at[5 + d])
        for d in range(2)
    ]
    edge_cot = [
        pltpu.make_async_copy(obj_hbm.at[d, 0], c4.at[span(2 + d)], local_sem.at[7 + d])
        for d in range(2)
    ]

    @pl.when(first)
    def _():
        for copy in edge_in:
            copy.start()

    @pl.when(last)
    def _():
        for copy in edge_cot:
            copy.start()

    pl.semaphore_wait(barrier, 4 + (groups - 1))

    piece = rows // CHUNKS

    def w_rows(owner, k):
        return w.at[pl.ds(pl.multiple_of(owner * rows + k * piece, piece), piece)]

    outgoing = []
    for k in range(CHUNKS):
        for j in range(1, groups):
            copy = remote(
                w_hbm.at[0, pl.ds(k * piece, piece)],
                w_rows(r, k),
                w_send.at[0, j, k],
                w_recv.at[0, j, k],
                dp=dp_at(j),
            )
            copy.start()
            outgoing.append(copy)

    mirror_first = [
        (kept_hbm.at[1, 0, 0], k4.at[span(1)]),
        (adj_hbm.at[1, 0], c4.at[span(1)]),
        (kept_hbm.at[1, 1, 0], k4.at[span(3)]),
    ]
    mirror = [
        remote(src, dst, mir_send.at[i], mir_recv.at[i], section=opposite)
        for i, (src, dst) in enumerate(mirror_first)
    ]
    for copy in mirror:
        copy.start()
    for k in range(CHUNKS):
        copy = remote(
            w_hbm.at[0, pl.ds(k * piece, piece)],
            w_rows(r, k),
            w_send.at[1, 0, k],
            w_recv.at[1, 0, k],
            dp=partner,
        )
        copy.start()
        outgoing.append(copy)
    for k in range(CHUNKS):
        for j in range(1, groups):
            source = 2 * lax.rem(h + groups - j, groups) + c
            arrived = w_rows(source, k)
            remote(arrived, arrived, w_send.at[0, j, k], w_recv.at[0, j, k], dp=source).wait_recv()
            copy = remote(
                arrived, arrived, w_send.at[1, j, k], w_recv.at[1, j, k], dp=partner
            )
            copy.start()
            outgoing.append(copy)
    for copy in local:
        copy.wait()
    for k in range(CHUNKS):
        for j in range(groups):
            source = 2 * lax.rem(h + groups - j, groups) + (1 - c)
            arrived = w_rows(source, k)
            remote(arrived, arrived, w_send.at[1, j, k], w_recv.at[1, j, k], dp=partner).wait_recv()

    col, f_tiles = tiles_of(ff, 256)
    wide, h_tiles = tiles_of(features, 256)

    def normalize(src, start, count, dst, dst_start, keep):
        step = 16

        def body(i, carry):
            at = pl.ds(pl.multiple_of(start + i * step, step), step)
            to = pl.ds(pl.multiple_of(dst_start + i * step, step), step)
            values = src[at, :].astype(F32)
            inverse = lax.rsqrt(jnp.mean(values * values, axis=-1, keepdims=True) + 1e-06)
            dst[to, :] = (values * inverse).astype(BF16)
            if keep:
                inv_ref[pl.ds(pl.multiple_of(i * step, step), step), :] = inverse
            return carry

        lax.fori_loop(0, count // step, body, 0)

    def dot(a, b):
        return jnp.dot(a, b, preferred_element_type=F32)

    def dot_t(a, b):
        return lax.dot_general(a, b, (((1,), (1,)), ((), ())), preferred_element_type=F32)

    def forward(start, count, out_start):
        at = pl.ds(start, count)
        normalize(x4, start, count, fn, 0, False)
        here = pl.ds(0, count)

        def up(j, carry):
            gate_part = dot(fn[here, :], w[:, pl.ds(pl.multiple_of(j * col, col), col)])
            up_part = dot(fn[here, :], w[:, pl.ds(pl.multiple_of(ff + j * col, col), col)])
            fh[here, pl.ds(pl.multiple_of(j * col, col), col)] = (
                gate_part * jax.nn.sigmoid(gate_part) * up_part
            ).astype(BF16)
            return carry

        lax.fori_loop(0, f_tiles, up, 0)

        def down(j, carry):
            lanes = pl.ds(pl.multiple_of(j * wide, wide), wide)
            branch = dot_t(fh[here, :], w[lanes, 2 * ff :])
            o6[pl.ds(out_start, count), lanes] = (x4[at, lanes].astype(F32) + branch).astype(BF16)
            return carry

        lax.fori_loop(0, h_tiles, down, 0)

    def reverse(slot, out_slot):
        at = span(slot)
        normalize(k4, slot * tokens, tokens, n4, slot * tokens, True)

        def up(j, carry):
            lanes = pl.ds(pl.multiple_of(j * col, col), col)
            beyond = pl.ds(pl.multiple_of(ff + j * col, col), col)
            gate_part = dot(n4[at, :], w[:, lanes])
            up_part = dot(n4[at, :], w[:, beyond])
            hidden_grad = dot(c4[at, :], w[:, pl.ds(pl.multiple_of(2 * ff + j * col, col), col)])
            sigmoid_gate = jax.nn.sigmoid(gate_part)
            silu_gate = gate_part * sigmoid_gate
            h4[at, lanes] = (silu_gate * up_part).astype(BF16)
            p4[at, lanes] = (
                hidden_grad * up_part * sigmoid_gate * (1.0 + gate_part * (1.0 - sigmoid_gate))
            ).astype(BF16)
            p4[at, beyond] = (hidden_grad * silu_gate).astype(BF16)
            return carry

        lax.fori_loop(0, f_tiles, up, 0)
        if out_slot is None:
            return

        def back(j, total):
            lanes = pl.ds(pl.multiple_of(j * wide, wide), wide)
            grad = dot_t(p4[at, :], w[lanes, : 2 * ff])
            g_ref[:, lanes] = grad
            return total + jnp.sum(grad * k4[at, lanes].astype(F32), axis=-1, keepdims=True)

        total = lax.fori_loop(0, h_tiles, back, jnp.zeros((tokens, 1), F32))
        inverse = inv_ref[...]
        scale = inverse * inverse * inverse * (total / features)

        def finish(j, carry):
            lanes = pl.ds(pl.multiple_of(j * wide, wide), wide)
            o6[span(out_slot), lanes] = (
                c4[at, lanes].astype(F32)
                + inverse * g_ref[:, lanes]
                - k4[at, lanes].astype(F32) * scale
            ).astype(BF16)
            return carry

        lax.fori_loop(0, h_tiles, finish, 0)

    def weight_rows(q, store):
        size, count = tiles_of(rows, 256)
        for t in range(count):
            lanes = pl.ds(pl.multiple_of(q * rows + t * size, size), size)
            left, left_cot = n4[:, lanes], c4[:, lanes]
            across = (((0,), (0,)), ((), ()))

            def inward(j, carry):
                out = pl.ds(pl.multiple_of(j * col, col), col)
                store(
                    pl.ds(t * size, size),
                    out,
                    lax.dot_general(left, p4[:, out], across, preferred_element_type=F32),
                )
                return carry

            lax.fori_loop(0, 2 * f_tiles, inward, 0)

            def outward(j, carry):
                lanes_in = pl.ds(pl.multiple_of(j * col, col), col)
                out = pl.ds(pl.multiple_of(2 * ff + j * col, col), col)
                store(
                    pl.ds(t * size, size),
                    out,
                    lax.dot_general(left_cot, h4[:, lanes_in], across, preferred_element_type=F32),
                )
                return carry

            lax.fori_loop(0, f_tiles, outward, 0)

    def send_pass(i, src, dst, step):
        to = s + step
        copy = remote(src, dst, pass_send.at[i], pass_recv.at[i], section=to)
        inside = s < n_sec - 1 if step > 0 else s > 0

        @pl.when(inside)
        def _():
            copy.start()

    def recv_pass(i, dst, step, edge):
        outside = first if step > 0 else last
        copy = remote(dst, dst, pass_send.at[i], pass_recv.at[i], section=s)

        @pl.when(jnp.logical_not(outside))
        def _():
            copy.wait_recv()

        if edge is not None:

            @pl.when(outside)
            def _():
                edge.wait()

    half = tokens // HALVES
    reverse(0, 2)
    send_pass(0, o6.at[span(2)], c4.at[span(2)], -1)
    forward(0, tokens, 0)
    send_pass(2, o6.at[span(0)], x4.at[span(2)], 1)
    mirror[0].wait_recv()
    mirror[1].wait_recv()
    reverse(1, 3)
    send_pass(1, o6.at[span(3)], c4.at[span(3)], -1)
    mirror_x = []
    for i in range(HALVES):
        copy = remote(
            x_hbm.at[1, 0, pl.ds(i * half, half)],
            x4.at[pl.ds(tokens + i * half, half)],
            mir_send.at[3 + i],
            mir_recv.at[3 + i],
            section=opposite,
        )
        copy.start()
        mirror_x.append(copy)
    recv_pass(2, x4.at[span(2)], 1, edge_in[0])
    forward(2 * tokens, tokens, 4 * tokens)
    down_out = pltpu.make_async_copy(o6.at[span(4)], ahead_hbm.at[0, 0], out_sem.at[0])
    down_out.start()
    recv_pass(0, c4.at[span(2)], -1, edge_cot[0])
    reverse(2, None)
    mirror[2].wait_recv()
    recv_pass(1, c4.at[span(3)], -1, edge_cot[1])
    reverse(3, None)

    reduce_copies = []
    for j in range(groups):
        g = lax.rem(h + j, groups)

        def to_partner(at, lanes, value, j=j):
            part_send[j, at, lanes] = value.astype(BF16)

        weight_rows(2 * g + (1 - c), to_partner)
        copy = remote(
            part_send.at[j], part_recv.at[j], red_send.at[0, j], red_recv.at[0, j], dp=partner
        )
        copy.start()
        reduce_copies.append(copy)
    step, count = tiles_of(rows, 32)
    for j in list(range(1, groups)) + [0]:
        g = lax.rem(h + j, groups)

        def to_own(at, lanes, value, j=j):
            own[j, at, lanes] = value

        weight_rows(2 * g + c, to_own)
    for j in range(1, groups):
        reduce_copies[j].wait_recv()

        def add(i, carry, j=j):
            at = pl.ds(pl.multiple_of(i * step, step), step)
            y_send[j - 1, at, :] = (own[j, at, :] + part_recv[j, at, :].astype(F32)).astype(BF16)
            return carry

        lax.fori_loop(0, count, add, 0)
        copy = remote(
            y_send.at[j - 1], y_recv.at[j - 1], red_send.at[1, j], red_recv.at[1, j], dp=dp_at(j)
        )
        copy.start()
        reduce_copies.append(copy)
    for i in range(HALVES):
        mirror_x[i].wait_recv()
        forward(tokens + i * half, half, tokens + i * half)
        send_pass(
            3 + i,
            o6.at[pl.ds(tokens + i * half, half)],
            x4.at[pl.ds(3 * tokens + i * half, half)],
            1,
        )
    returned = []
    for i in range(HALVES):
        recv_pass(
            3 + i, x4.at[pl.ds(3 * tokens + i * half, half)], 1, edge_in[1] if i == 0 else None
        )
        forward(3 * tokens + i * half, half, 5 * tokens + i * half)
        copy = remote(
            o6.at[pl.ds(5 * tokens + i * half, half)],
            ahead_hbm.at[1, 0, pl.ds(i * half, half)],
            mir_send.at[3 + HALVES + i],
            mir_recv.at[3 + HALVES + i],
            section=opposite,
        )
        copy.start()
        returned.append(copy)
    reduce_copies[0].wait_recv()
    for copy in reduce_copies[groups:]:
        copy.wait_recv()

    def final(i, carry):
        at = pl.ds(pl.multiple_of(i * step, step), step)
        total = own[0, at, :] + part_recv[0, at, :].astype(F32)
        for j in range(1, groups):
            total = total + y_recv[j - 1, at, :].astype(F32)
        grad_out[at, :] = total
        return carry

    lax.fori_loop(0, count, final, 0)
    grad_copy = pltpu.make_async_copy(grad_out, grads_hbm.at[0], out_sem.at[1])
    grad_copy.start()
    for copy in returned:
        copy.wait_recv()

    for copy in outgoing + mirror + mirror_x + returned + reduce_copies:
        copy.wait_send()

    def drain(i, size, step):
        inside = s < n_sec - 1 if step > 0 else s > 0
        view = o6.at[pl.ds(0, size)]

        @pl.when(inside)
        def _():
            remote(view, view, pass_send.at[i], pass_recv.at[i], section=s).wait_send()

    drain(0, tokens, -1)
    drain(1, tokens, -1)
    drain(2, tokens, 1)
    for i in range(HALVES):
        drain(3 + i, half, 1)
    down_out.wait()
    grad_copy.wait()


def on_device(n_sec, n_dp, *arrays):
    x, inc, adj, obj, kept, weights = arrays
    _, _, tokens, features = x.shape
    _, rows, width = weights.shape
    ff, groups = width // 3, n_dp // 2
    dma = pltpu.SemaphoreType.DMA
    anywhere = pl.BlockSpec(memory_space=pl.ANY)
    return pl.pallas_call(
        functools.partial(kernel, n_sec, n_dp),
        out_shape=(
            jax.ShapeDtypeStruct(x.shape, BF16),
            jax.ShapeDtypeStruct(weights.shape, F32),
        ),
        in_specs=[anywhere] * 6,
        out_specs=(anywhere, anywhere),
        scratch_shapes=[
            pltpu.VMEM((features, width), BF16),
            pltpu.VMEM((4 * tokens, features), BF16),
            pltpu.VMEM((4 * tokens, features), BF16),
            pltpu.VMEM((4 * tokens, features), BF16),
            pltpu.VMEM((4 * tokens, features), BF16),
            pltpu.VMEM((4 * tokens, 2 * ff), BF16),
            pltpu.VMEM((4 * tokens, ff), BF16),
            pltpu.VMEM((6 * tokens, features), BF16),
            pltpu.VMEM((tokens, features), BF16),
            pltpu.VMEM((tokens, ff), BF16),
            pltpu.VMEM((tokens, 1), F32),
            pltpu.VMEM((tokens, features), F32),
            pltpu.VMEM((groups, rows, width), BF16),
            pltpu.VMEM((groups, rows, width), BF16),
            pltpu.VMEM((groups, rows, width), F32),
            pltpu.VMEM((groups - 1, rows, width), BF16),
            pltpu.VMEM((groups - 1, rows, width), BF16),
            pltpu.VMEM((rows, width), F32),
            dma((9,)),
            dma((2, groups, CHUNKS)),
            dma((2, groups, CHUNKS)),
            dma((3 + 2 * HALVES,)),
            dma((3 + 2 * HALVES,)),
            dma((3 + HALVES,)),
            dma((3 + HALVES,)),
            dma((2, groups)),
            dma((2, groups)),
            dma((2,)),
        ],
        compiler_params=pltpu.CompilerParams(
            collective_id=0, has_side_effects=True, vmem_limit_bytes=60 * 1024 * 1024
        ),
    )(x, inc, adj, obj, kept, weights)


def solution(mesh):
    in_specs = (
        P(None, "dp", "section", None),
        P(None, "dp", None, None),
        P(None, "dp", "section", None),
        P(None, "dp", None, None),
        P(None, None, "dp", "section", None),
        P("section", "dp", None),
    )
    out_specs = (P(None, "dp", "section", None), P("section", "dp", None))
    body = functools.partial(on_device, mesh.shape["section"], mesh.shape["dp"])
    return jax.shard_map(
        body, mesh=mesh, in_specs=in_specs, out_specs=out_specs, check_vma=False
    )
```

time: 227 us -> 184 us (0.81)
  the two profiles are of different devices: /device:TPU:21 before, /device:TPU:18 now
where the time goes in v2:
time: 184 us
  Pallas kernels  177 us (96%)
  local copies, waits for them, and re-layouts  6.06 us (3%)
    pallas_call x1, Pallas kernels, on_device(): pl.pallas_call(functools.partial(kernel, n_sec, n_dp), out_shape=(jax.Sha...  177 us
    unnamed x2, local copies, waits for them, and re-layouts  6.06 us

profile of v2, /device:TPU:18, one launch (start us, length us, event | category | flops | bytes accessed | tf_op | source)
XLA Modules:
  0.0 183.7 jit_solution(3224646233448160743)
XLA Ops:
  0.6 177.0 %shard_map.77 = (bf16[2,1,128,2048]{3,2,1,0:T(8,128)(2,1)}, f32[1,512,1536]{2,1,0:T(8,128)}) custom-call(bf16[2,1,128,2048]{3,2,1,0:T(8,128)(2,1)} %x_hbm.1, bf16[2,1,128,2048]{3,2,1,0:T(8,128)(2,1)} %inc_hbm.1, bf16[2,1,128,2048]{3,2,1,0:T(8,128)(2,1)} %adj_hbm.1, bf16[2,1,128,2048]{3,2,1,0:T(8,128)(2,1)} %obj_hbm.1, ...), custom_call_target="tpu_custom_call" | custom-call | tf_op jit(solution)/shard_map/pallas_call | solution.py:467
  177.7 2.3 %copy.10 = bf16[2,1,128,2048]{3,2,1,0:T(8,128)(2,1)} copy(bf16[2,1,128,2048]{3,2,1,0:T(8,128)(2,1)} %get-tuple-element.4) | data formatting | bytes 2097152
  180.0 3.8 %copy.11 = f32[1,512,1536]{2,1,0:T(8,128)} copy(f32[1,512,1536]{2,1,0:T(8,128)} %get-tuple-element.5) | data formatting | bytes 6291456

commit v3 on v2

--- a/solution.py
+++ b/solution.py
@@ -86,6 +86,8 @@
     def span(block, size=tokens):
         return pl.ds(block * size, size)
 
+    half = tokens // HALVES
+
     barrier = pltpu.get_barrier_semaphore()
 
     def greet(**where):
@@ -330,7 +332,6 @@
             def _():
                 edge.wait()
 
-    half = tokens // HALVES
     reverse(0, 2)
     send_pass(0, o6.at[span(2)], c4.at[span(2)], -1)
     forward(0, tokens, 0)
@@ -339,6 +340,13 @@
     mirror[1].wait_recv()
     reverse(1, 3)
     send_pass(1, o6.at[span(3)], c4.at[span(3)], -1)
+    recv_pass(2, x4.at[span(2)], 1, edge_in[0])
+    forward(2 * tokens, tokens, 4 * tokens)
+    down_out = pltpu.make_async_copy(o6.at[span(4)], ahead_hbm.at[0, 0], out_sem.at[0])
+    down_out.start()
+    recv_pass(0, c4.at[span(2)], -1, edge_cot[0])
+    reverse(2, None)
+    mirror[2].wait_recv()
     mirror_x = []
     for i in range(HALVES):
         copy = remote(
@@ -350,18 +358,11 @@
         )
         copy.start()
         mirror_x.append(copy)
-    recv_pass(2, x4.at[span(2)], 1, edge_in[0])
-    forward(2 * tokens, tokens, 4 * tokens)
-    down_out = pltpu.make_async_copy(o6.at[span(4)], ahead_hbm.at[0, 0], out_sem.at[0])
-    down_out.start()
-    recv_pass(0, c4.at[span(2)], -1, edge_cot[0])
-    reverse(2, None)
-    mirror[2].wait_recv()
     recv_pass(1, c4.at[span(3)], -1, edge_cot[1])
     reverse(3, None)
 
-    reduce_copies = []
-    for j in range(groups):
+    reduce_copies = [None] * groups
+    for j in list(range(1, groups)) + [0]:
         g = lax.rem(h + j, groups)
 
         def to_partner(at, lanes, value, j=j):
@@ -372,7 +373,7 @@
             part_send.at[j], part_recv.at[j], red_send.at[0, j], red_recv.at[0, j], dp=partner
         )
         copy.start()
-        reduce_copies.append(copy)
+        reduce_copies[j] = copy
     step, count = tiles_of(rows, 32)
     for j in list(range(1, groups)) + [0]:
         g = lax.rem(h + j, groups)

time: 184 us -> 178 us (0.967)
  the two profiles are of different devices: /device:TPU:18 before, /device:TPU:21 now
where the time goes in v3:
time: 178 us; the launch traced here: 177 us
  Pallas kernels  170 us (96%)
  local copies, waits for them, and re-layouts  6.06 us (3%)
    pallas_call x1, Pallas kernels, on_device(): pl.pallas_call(functools.partial(kernel, n_sec, n_dp), out_shape=(jax.Sha...  170 us
    unnamed x2, local copies, waits for them, and re-layouts  6.06 us

profile of v3, /device:TPU:21, one launch (start us, length us, event | category | flops | bytes accessed | tf_op | source)
XLA Modules:
  0.0 176.6 jit_solution(4434057634199750454)
XLA Ops:
  0.6 169.9 %shard_map.77 = (bf16[2,1,128,2048]{3,2,1,0:T(8,128)(2,1)}, f32[1,512,1536]{2,1,0:T(8,128)}) custom-call(bf16[2,1,128,2048]{3,2,1,0:T(8,128)(2,1)} %x_hbm.1, bf16[2,1,128,2048]{3,2,1,0:T(8,128)(2,1)} %inc_hbm.1, bf16[2,1,128,2048]{3,2,1,0:T(8,128)(2,1)} %adj_hbm.1, bf16[2,1,128,2048]{3,2,1,0:T(8,128)(2,1)} %obj_hbm.1, ...), custom_call_target="tpu_custom_call" | custom-call | tf_op jit(solution)/shard_map/pallas_call | solution.py:468
  170.5 2.3 %copy.10 = bf16[2,1,128,2048]{3,2,1,0:T(8,128)(2,1)} copy(bf16[2,1,128,2048]{3,2,1,0:T(8,128)(2,1)} %get-tuple-element.4) | data formatting | bytes 2097152
  172.8 3.8 %copy.11 = f32[1,512,1536]{2,1,0:T(8,128)} copy(f32[1,512,1536]{2,1,0:T(8,128)} %get-tuple-element.5) | data formatting | bytes 6291456
